TPU v7x, 32 devices: a whole 2x2x4 slice. The times are simulated.
32 devices in a mesh: parts: 2 (over y), tmpl: 4 (over z), sta: 4 (over x, core).
Axes of the slice: x: 2, y: 2, z: 4, core: 2. Of those that a mesh axis runs over, the one named last changes fastest.
Arguments:
- data: float32 [64, 3, 1280], P(('parts', 'sta'), None, 'tmpl'), parts along dimension 0, as said below
- templates: bfloat16 [32, 3, 16, 256], P('sta', None, 'tmpl'), as said below
- starts: int32 [32, 3, 16], P('sta', None, 'tmpl'), may hold values from 0 to 512
Outputs:
- network: float32 [32, 512], P(('parts', 'tmpl'), 'sta'), parts along dimension 0
There are 2 independent parts, one for each index of `parts`. A program takes and returns all parts, laid end to end along the dimension named above; an argument that names none is the same for every part. Nothing has to cross between parts.
Inputs may be any that keep to these rules, and one draw needn't show every extreme that they name: `data`: finite samples. `templates`: finite samples.
All inputs are finite; a program needn't handle non-finite values.
Results may differ from a plain program's by a relative error of at most 0.0029.
Values sent between devices are 32-bit elements; how exact they have to be, the bound alone decides.
A program may use at most 64 MiB of HBM per device.

v0:
```python
import jax
import jax.numpy as jnp
from jax import lax
from jax.sharding import PartitionSpec as P

TLEN = 256
MAXSHIFT = 512
LAGS = 512


EPS = 1e-06


def window_energy(trace):
    extent = LAGS + MAXSHIFT
    squares = trace * trace
    running = jnp.concatenate([jnp.zeros_like(squares[:, :1]), jnp.cumsum(squares, axis=1)], axis=1)
    return running[:, TLEN : TLEN + extent] - running[:, :extent]


def take_window(row, offset):
    return lax.dynamic_slice_in_dim(row, offset, LAGS, 0)


def local_term(whole, templates, starts):
    extent = LAGS + MAXSHIFT
    stations, channels, samples = whole.shape
    per_group = templates.shape[2]
    groups = stations * channels
    lowered = whole.astype(jnp.bfloat16).reshape(1, groups, samples)
    kernel = templates.reshape(groups * per_group, 1, templates.shape[-1])
    raw = lax.conv_general_dilated(
        lowered,
        kernel,
        (1,),
        "VALID",
        dimension_numbers=("NCH", "OIH", "NCH"),
        feature_group_count=groups,
        preferred_element_type=jnp.float32,
    )[0]
    raw = raw[:, :extent]
    energy = window_energy(whole.reshape(groups, samples))
    energy_rows = jnp.repeat(energy, per_group, axis=0)
    tnorm = jnp.sum(jnp.square(templates.astype(jnp.float32)), axis=-1).reshape(-1)
    offsets = starts.reshape(-1)
    slicer = jax.vmap(take_window)
    aligned = slicer(raw, offsets)
    local = slicer(energy_rows, offsets)
    scale = TLEN * jnp.sqrt((tnorm[:, None] / TLEN + EPS) * (local / TLEN + EPS))
    return jnp.sum((aligned / scale).reshape(groups, per_group, LAGS), axis=0)


def shards(data, templates, starts):
    whole = lax.all_gather(data, "tmpl", axis=2, tiled=True)
    partial_value = local_term(whole, templates, starts)
    summed = lax.psum(partial_value, "sta")
    width = LAGS // lax.axis_size("sta")
    return lax.dynamic_slice_in_dim(summed, lax.axis_index("sta") * width, width, 1)


def solution(mesh):
    return jax.shard_map(
        shards,
        mesh=mesh,
        in_specs=(
            P(("parts", "sta"), None, "tmpl"),
            P("sta", None, "tmpl", None),
            P("sta", None, "tmpl"),
        ),
        out_specs=P(("parts", "tmpl"), "sta"),
        check_vma=False,
    )
```

profile of v0, /device:TPU:0, one launch (start us, length us, event | category | flops | bytes accessed | tf_op | source)
XLA Modules:
  0.0 490.5 jit_solution(16499657202032533554)
XLA Ops:
  1.0 47.9 %all_gather.3 = f32[8,3,1280]{0,1,2:T(4,128)S(1)} all-gather(f32[8,3,320]{0,1,2:T(4,128)S(1)} %copy.29), channel_id=1, replica_groups=mesh['parts'=2,'tmpl'=4,'sta'=4] {'tmpl'}, dimensions={2}, use_global_device_ids=true | all-gather | bytes 153600 | tf_op jit(solution)/shard_map/all_gather | solution.py:54
  49.9 6.8 %reduce-window.6 = f32[24,10,128]{2,1,0:T(8,128)S(1)} reduce-window(f32[24,10,128]{2,1,0:T(8,128)S(1)} %mul.25, f32[]{:T(128)} %constant.9.clone.1), window={size=1x1x128 pad=0_0x0_0x127_0}, to_apply=%region_1.2 | reduce-window | flops 3901440 | bytes 245764 | tf_op jit(solution)/shard_map/reduce-window
  58.0 197.6 %while.3 = (s32[]{:T(128)}, f32[96,1024]{1,0:T(8,128)S(1)}, s32[96,2]{0,1:T(2,128)S(1)}, f32[96,512]{1,0:T(8,128)S(1)}, s32[]{:T(128)}, /*index=5*/s32[]{:T(128)}) while((s32[]{:T(128)}, f32[96,1024]{1,0:T(8,128)S(1)}, s32[96,2]{0,1:T(2,128)S(1)}, f32[96,512]{1,0:T(8,128)S(1)}, s32[]{:T(128)}, /*index=5*/s32[]{:T(128)}) %tuple.38), condition=%wide.while_cond.1, body=%wide.while_body.1.sunk | while | flops 2 | bytes 8305 | solution.py:22
  58.7 1.3 dynamic-slice.15
  60.8 1.3 dynamic-slice.15
  62.8 1.3 dynamic-slice.15
  64.9 1.3 dynamic-slice.15
  66.9 1.3 dynamic-slice.15
  89.6 1.3 dynamic-slice.15
  91.6 1.3 dynamic-slice.15
  93.7 1.3 dynamic-slice.15
  95.8 1.3 dynamic-slice.15
  97.8 1.3 dynamic-slice.15
  99.9 1.3 dynamic-slice.15
  101.9 1.3 dynamic-slice.15
  104.0 1.3 dynamic-slice.15
  106.0 1.3 dynamic-slice.15
  128.7 1.3 dynamic-slice.15
  130.7 1.3 dynamic-slice.15
  132.8 1.3 dynamic-slice.15
  134.9 1.3 dynamic-slice.15
  136.9 1.3 dynamic-slice.15
  139.0 1.3 dynamic-slice.15
  141.0 1.3 dynamic-slice.15
  143.1 1.3 dynamic-slice.15
  145.2 1.3 dynamic-slice.15
  167.8 1.3 dynamic-slice.15
  169.9 1.3 dynamic-slice.15
  171.9 1.3 dynamic-slice.15
  256.5 28.5 %fusion.1 = f32[1,96,1025]{1,0,2:T(1,128)S(1)} fusion(bf16[1,24,1280]{1,0,2:T(2,128)(2,1)S(1)} %copy.33, s32[96]{0:T(128)S(1)} %copy-done.2, bf16[96,256]{0,1:T(8,128)(2,1)S(1)} %copy.32), kind=kOutput, calls=%fused_computation.4 | convolution fusion | flops 1210318848 | bytes 504576 | tf_op jit(solution)/shard_map/conv_general_dilated | solution.py:32
  285.8 197.6 %while.2 = (s32[]{:T(128)}, f32[96,1024]{1,0:T(8,128)S(1)}, s32[96,2]{0,1:T(2,128)S(1)}, f32[96,512]{1,0:T(8,128)S(1)}, s32[]{:T(128)}, /*index=5*/s32[]{:T(128)}) while((s32[]{:T(128)}, f32[96,1024]{1,0:T(8,128)S(1)}, s32[96,2]{0,1:T(2,128)S(1)}, f32[96,512]{1,0:T(8,128)S(1)}, s32[]{:T(128)}, /*index=5*/s32[]{:T(128)}) %tuple.41), condition=%wide.while_cond, body=%wide.while_body.sunk | while | flops 2 | bytes 8305 | solution.py:22
  484.1 5.8 %psum.7 = f32[4,512]{1,0:T(4,128)S(1)} all-reduce(f32[4,512]{1,0:T(4,128)S(1)} %fusion.5), channel_id=1, replica_groups=mesh['parts'=2,'tmpl'=4,'sta'=4] {'sta'}, use_global_device_ids=true, to_apply=%region_4.5 | all-reduce | flops 2048 | bytes 16384 | tf_op jit(solution)/shard_map/psum | solution.py:56
  (786 shorter events, 362.2 us)
Async XLA Ops:
  56.7 1.0 copy-start.1
  57.6 198.7 %copy-start = (bf16[8,3,4,256]{3,2,1,0:T(4,128)(2,1)S(1)}, bf16[8,3,4,256]{3,2,1,0:T(4,128)(2,1)}, u32[]{:S(2)}) copy-start(bf16[8,3,4,256]{3,2,1,0:T(4,128)(2,1)} %param.4) | copy-start | bytes 147460
  57.6 198.9 %copy-start.2 = (s32[96]{0:T(128)S(1)}, s32[96]{0:T(128)}, u32[]{:S(2)}) copy-start(s32[96]{0:T(128)} %constant.11.clone.1) | copy-start | bytes 1156
where the time goes:
time: 494 us; the launch traced here: 490 us
  local copies, waits for them, and re-layouts  396 us (80%)
  blocking collectives  53.7 us (11%)
  matrix products  28.5 us (6%)
  other arithmetic  7.52 us (2%)
    gather x768, local copies, waits for them, and re-layouts  391 us
    all_gather x1, blocking collectives, shards(): whole = lax.all_gather(data, 'tmpl', axis=2, tiled=True)  47.9 us
    conv_general_dilated x1, matrix products, local_term(): lax.conv_general_dilated(lowered, kernel, (1,), 'VALID', dimension_number...  28.5 us

commit v1 on v0

v1 whole, which is shorter than its diff:
```python
import functools

import jax
import jax.numpy as jnp
from jax import lax
from jax.experimental import pallas as pl
from jax.experimental.pallas import tpu as pltpu
from jax.sharding import PartitionSpec as P

TLEN = 256
MAXSHIFT = 512
LAGS = 512
EXTENT = LAGS + MAXSHIFT
LANE = 128
CHUNKS = EXTENT // LANE
BAND = TLEN + LANE
ROWS = 16
EPS = 1e-06

MESH = pl.DeviceIdType.MESH


def kernel(
    peers, owners,
    starts_hbm, data_ref, templates_hbm, out_ref,
    starts_ref, templates_ref, local_sems, gathered, chunked, flat, bands, norms, inverse, lagged, partial_ref, arrived,
    data_send, data_recv, sum_send, sum_recv,
):
    channels, stations, width = data_ref.shape
    per_group = templates_ref.shape[2]
    groups = stations * channels
    samples = width * peers
    my_tmpl = lax.axis_index("tmpl")
    my_sta = lax.axis_index("sta")

    fetches = [
        pltpu.make_async_copy(templates_hbm, templates_ref, local_sems.at[0]),
        pltpu.make_async_copy(starts_hbm, starts_ref, local_sems.at[1]),
        pltpu.make_async_copy(data_ref, gathered.at[my_tmpl], local_sems.at[2]),
    ]
    for copy in fetches:
        copy.start()

    barrier = pltpu.get_barrier_semaphore()
    for step in range(1, peers):
        pl.semaphore_signal(
            barrier, inc=1, device_id={"tmpl": lax.rem(my_tmpl + step, peers)}, device_id_type=MESH
        )
    for step in range(1, owners):
        pl.semaphore_signal(
            barrier, inc=1, device_id={"sta": lax.rem(my_sta + step, owners)}, device_id_type=MESH
        )
    pl.semaphore_wait(barrier, peers + owners - 2)

    sends = []
    for step in range(1, peers):
        copy = pltpu.make_async_remote_copy(
            src_ref=data_ref,
            dst_ref=gathered.at[my_tmpl],
            send_sem=data_send.at[step],
            recv_sem=data_recv.at[my_tmpl],
            device_id={"tmpl": lax.rem(my_tmpl + step, peers)},
            device_id_type=MESH,
        )
        copy.start()
        sends.append(copy)
    fetches[0].wait()

    for s in range(stations):
        for c in range(channels):
            row = (s * channels + c) * per_group
            flat[row : row + per_group, :] = templates_ref[s, c].astype(jnp.float32)
    waves = flat[...]
    tnorm = jnp.sum(waves * waves, axis=1, keepdims=True)
    norms[...] = jnp.broadcast_to(lax.rsqrt(tnorm / TLEN + EPS) / TLEN, norms.shape)
    down = lax.broadcasted_iota(jnp.int32, (TLEN, TLEN), 0)
    across = lax.broadcasted_iota(jnp.int32, (TLEN, TLEN), 1)
    flip = jnp.where(down + across == TLEN - 1, 1.0, 0.0).astype(jnp.bfloat16)
    flat[...] = jnp.dot(waves.astype(jnp.bfloat16), flip, preferred_element_type=jnp.float32)

    sub = lax.broadcasted_iota(jnp.int32, (8, LANE), 0)
    lane = lax.broadcasted_iota(jnp.int32, (8, LANE), 1)

    def build(group, carry):
        for t in range(per_group):
            row = flat[pl.ds(group * per_group + t, 1), :]
            low = jnp.broadcast_to(row[:, :LANE], (8, LANE))
            high = jnp.broadcast_to(row[:, LANE:], (8, LANE))
            low = pltpu.roll(low, 1, 1, stride=1, stride_axis=0)
            high = pltpu.roll(high, 1, 1, stride=1, stride_axis=0)
            for pair in range(LANE // 16):
                parts = [[], [], []]
                for q in (2 * pair, 2 * pair + 1):
                    keep = lane <= sub + 8 * q
                    first = pltpu.roll(low, 8 * q, 1) if q else low
                    second = pltpu.roll(high, 8 * q, 1) if q else high
                    parts[0].append(jnp.where(keep, second, 0.0))
                    parts[1].append(jnp.where(keep, first, second))
                    parts[2].append(jnp.where(keep, 0.0, first))
                for block in range(3):
                    top = block * LANE + pair * 16
                    bands[group, top : top + 16, t * LANE : (t + 1) * LANE] = jnp.concatenate(
                        parts[block], axis=0
                    ).astype(jnp.bfloat16)
        return carry

    lax.fori_loop(0, groups, build, 0)

    fetches[1].wait()
    fetches[2].wait()
    for step in range(1, peers):
        source = lax.rem(my_tmpl + peers - step, peers)
        pltpu.make_async_remote_copy(
            src_ref=data_ref,
            dst_ref=gathered.at[source],
            send_sem=data_send.at[step],
            recv_sem=data_recv.at[source],
            device_id={"tmpl": source},
            device_id_type=MESH,
        ).wait_recv()
    for c in range(channels):
        whole = jnp.concatenate([gathered[i, c] for i in range(peers)], axis=1)
        for j in range(samples // LANE):
            chunked[pl.ds(c * ROWS + j, stations, stride=channels * ROWS), :] = whole[
                :, j * LANE : (j + 1) * LANE
            ]

    def windows(group):
        return jnp.concatenate(
            [chunked[group * ROWS + i : group * ROWS + i + CHUNKS, :] for i in range(3)], axis=1
        )

    squares = []
    for group in range(groups):
        samples_in = windows(group)
        squares.append(samples_in * samples_in)
    squares = jnp.concatenate(squares, axis=0)
    upper = squares.astype(jnp.bfloat16)
    lower = (squares - upper.astype(jnp.float32)).astype(jnp.bfloat16)
    offset = lax.broadcasted_iota(jnp.int32, (BAND, LANE), 0) - lax.broadcasted_iota(
        jnp.int32, (BAND, LANE), 1
    )
    ones = jnp.where((offset >= 0) & (offset < TLEN), 1.0, 0.0).astype(jnp.bfloat16)
    energy = jnp.dot(upper, ones, preferred_element_type=jnp.float32) + jnp.dot(
        lower, ones, preferred_element_type=jnp.float32
    )
    inverse[...] = lax.rsqrt(energy / TLEN + EPS)

    for group in range(groups):
        raw = jnp.dot(
            windows(group).astype(jnp.bfloat16), bands[group], preferred_element_type=jnp.float32
        )
        local = inverse[group * CHUNKS : (group + 1) * CHUNKS, :]
        for t in range(per_group):
            row = group * per_group + t
            lagged[row, :CHUNKS, :] = raw[:, t * LANE : (t + 1) * LANE] * (
                local * norms[row : row + 1, :]
            )

    zero = jnp.zeros((CHUNKS, LANE), jnp.float32)
    for t in range(per_group):
        same, following = zero, zero
        for s in range(stations):
            for c in range(channels):
                start = starts_ref[c, t, s]
                chunk = start >> 7
                inside = start & (LANE - 1)
                row = (s * channels + c) * per_group + t
                moved = pltpu.roll(lagged[row, pl.ds(chunk, CHUNKS), :], (LANE - inside) & (LANE - 1), 1)
                keep = lane < LANE - inside
                same = same + jnp.where(keep, moved, 0.0)
                following = following + jnp.where(keep, 0.0, moved)
        rows = LAGS // LANE
        partial_ref[:, t, :] = same[:rows] + following[1 : rows + 1]

    span = LAGS // LANE // owners
    for step in range(1, owners):
        target = lax.rem(my_sta + step, owners)
        copy = pltpu.make_async_remote_copy(
            src_ref=partial_ref.at[pl.ds(target * span, span)],
            dst_ref=arrived.at[my_sta],
            send_sem=sum_send.at[step],
            recv_sem=sum_recv.at[my_sta],
            device_id={"sta": target},
            device_id_type=MESH,
        )
        copy.start()
        sends.append(copy)
    total = partial_ref[pl.ds(my_sta * span, span)]
    for step in range(1, owners):
        source = lax.rem(my_sta + owners - step, owners)
        pltpu.make_async_remote_copy(
            src_ref=partial_ref.at[pl.ds(source * span, span)],
            dst_ref=arrived.at[source],
            send_sem=sum_send.at[step],
            recv_sem=sum_recv.at[source],
            device_id={"sta": source},
            device_id_type=MESH,
        ).wait_recv()
        total = total + arrived[source]
    for i in range(span):
        out_ref[:, i * LANE : (i + 1) * LANE] = total[i]
    for copy in sends:
        copy.wait_send()


def shards(data, templates, starts):
    peers, owners = lax.axis_size("tmpl"), lax.axis_size("sta")
    stations, channels, width = data.shape
    per_group = templates.shape[2]
    groups = stations * channels
    vmem = pl.BlockSpec(memory_space=pltpu.VMEM)
    span = LAGS // LANE // owners
    return pl.pallas_call(
        functools.partial(kernel, peers, owners),
        out_shape=jax.ShapeDtypeStruct((per_group, LAGS // owners), jnp.float32),
        in_specs=[pl.BlockSpec(memory_space=pltpu.HBM)] * 3,
        out_specs=vmem,
        scratch_shapes=[
            pltpu.SMEM((channels, per_group, stations), jnp.int32),
            pltpu.VMEM(templates.shape, templates.dtype),
            pltpu.SemaphoreType.DMA((3,)),
            pltpu.VMEM((peers, channels, stations, width), jnp.float32),
            pltpu.VMEM((groups * ROWS, LANE), jnp.float32),
            pltpu.VMEM((groups * per_group, TLEN), jnp.float32),
            pltpu.VMEM((groups, BAND, per_group * LANE), jnp.bfloat16),
            pltpu.VMEM((groups * per_group, LANE), jnp.float32),
            pltpu.VMEM((groups * CHUNKS, LANE), jnp.float32),
            pltpu.VMEM((groups * per_group, ROWS, LANE), jnp.float32),
            pltpu.VMEM((LAGS // LANE, per_group, LANE), jnp.float32),
            pltpu.VMEM((owners, span, per_group, LANE), jnp.float32),
            pltpu.SemaphoreType.DMA((peers,)),
            pltpu.SemaphoreType.DMA((peers,)),
            pltpu.SemaphoreType.DMA((owners,)),
            pltpu.SemaphoreType.DMA((owners,)),
        ],
        compiler_params=pltpu.CompilerParams(
            collective_id=0, has_side_effects=True, vmem_limit_bytes=64 * 1024 * 1024
        ),
    )(jnp.transpose(starts, (1, 2, 0)), jnp.transpose(data, (1, 0, 2)), templates)


def solution(mesh):
    return jax.shard_map(
        shards,
        mesh=mesh,
        in_specs=(
            P(("parts", "sta"), None, "tmpl"),
            P("sta", None, "tmpl", None),
            P("sta", None, "tmpl"),
        ),
        out_specs=P(("parts", "tmpl"), "sta"),
        check_vma=False,
    )
```

time: 494 us -> 17.3 us (0.04)
  local copies, waits for them, and re-layouts: 396 us -> 1.26 us
  blocking collectives: 53.7 us -> 0 us
  matrix products: 28.5 us -> 0 us
  Pallas kernels: 0 us -> 15.9 us
  other arithmetic: 7.52 us -> 0 us
    gather x769 -> x0, local copies, waits for them, and re-layouts: 391 us -> none
    all_gather x1 -> x0, blocking collectives: 47.9 us -> none  [shards(): whole = lax.all_gather(data, 'tmpl', axis=2, tiled=True)]
    conv_general_dilated x1 -> x0, matrix products: 28.5 us -> none  [local_term(): lax.conv_general_dilated(lowered, kernel, (1,), 'VALID', dimension_number...]
    pallas_call x0 -> x1, Pallas kernels: none -> 15.9 us  [shards(): pl.pallas_call(functools.partial(kernel, peers, owners), out_shape=jax.Sh...]
    another operation x3 -> x0, other arithmetic: 6.96 us -> none
    psum x1 -> x0, blocking collectives: 5.77 us -> none  [shards(): summed = lax.psum(partial_value, 'sta')]
where the time goes in v1:
time: 17.3 us; the launch traced here: 17.1 us
  Pallas kernels  15.9 us (92%)
  local copies, waits for them, and re-layouts  1.26 us (7%)
    pallas_call x1, Pallas kernels, shards(): pl.pallas_call(functools.partial(kernel, peers, owners), out_shape=jax.Sh...  15.9 us
    unnamed x1, local copies, waits for them, and re-layouts  1.26 us

profile of v1, /device:TPU:0, one launch (start us, length us, event | category | flops | bytes accessed | tf_op | source)
XLA Modules:
  0.0 17.1 jit_solution(1139820095455373660)
XLA Ops:
  0.0 15.9 %shard_map.37 = f32[4,128]{1,0:T(4,128)} custom-call(s32[3,4,8]{2,1,0:T(4,128)} %bitcast.3, f32[3,8,320]{2,1,0:T(8,128)} %bitcast.2, bf16[8,3,4,256]{3,2,1,0:T(4,128)(2,1)} %templates_hbm.1), custom_call_target="tpu_custom_call" | custom-call | tf_op jit(solution)/shard_map/pallas_call | solution.py:214
  15.9 1.3 %copy.5 = f32[4,128]{1,0:T(4,128)} copy(f32[4,128]{1,0:T(4,128)} %shard_map.37) | data formatting | bytes 4096

commit v2 on v1

--- a/solution.py
+++ b/solution.py
@@ -50,33 +50,19 @@
         pl.semaphore_signal(
             barrier, inc=1, device_id={"sta": lax.rem(my_sta + step, owners)}, device_id_type=MESH
         )
-    pl.semaphore_wait(barrier, peers + owners - 2)
-
-    sends = []
-    for step in range(1, peers):
-        copy = pltpu.make_async_remote_copy(
-            src_ref=data_ref,
-            dst_ref=gathered.at[my_tmpl],
-            send_sem=data_send.at[step],
-            recv_sem=data_recv.at[my_tmpl],
-            device_id={"tmpl": lax.rem(my_tmpl + step, peers)},
-            device_id_type=MESH,
-        )
-        copy.start()
-        sends.append(copy)
-    fetches[0].wait()
-
-    for s in range(stations):
-        for c in range(channels):
-            row = (s * channels + c) * per_group
-            flat[row : row + per_group, :] = templates_ref[s, c].astype(jnp.float32)
-    waves = flat[...]
-    tnorm = jnp.sum(waves * waves, axis=1, keepdims=True)
-    norms[...] = jnp.broadcast_to(lax.rsqrt(tnorm / TLEN + EPS) / TLEN, norms.shape)
-    down = lax.broadcasted_iota(jnp.int32, (TLEN, TLEN), 0)
-    across = lax.broadcasted_iota(jnp.int32, (TLEN, TLEN), 1)
-    flip = jnp.where(down + across == TLEN - 1, 1.0, 0.0).astype(jnp.bfloat16)
-    flat[...] = jnp.dot(waves.astype(jnp.bfloat16), flip, preferred_element_type=jnp.float32)
+    def prepare():
+        fetches[0].wait()
+        for s in range(stations):
+            for c in range(channels):
+                row = (s * channels + c) * per_group
+                flat[row : row + per_group, :] = templates_ref[s, c].astype(jnp.float32)
+        waves = flat[...]
+        tnorm = jnp.sum(waves * waves, axis=1, keepdims=True)
+        norms[...] = jnp.broadcast_to(lax.rsqrt(tnorm / TLEN + EPS) / TLEN, norms.shape)
+        down = lax.broadcasted_iota(jnp.int32, (TLEN, TLEN), 0)
+        across = lax.broadcasted_iota(jnp.int32, (TLEN, TLEN), 1)
+        flip = jnp.where(down + across == TLEN - 1, 1.0, 0.0).astype(jnp.bfloat16)
+        flat[...] = jnp.dot(waves.astype(jnp.bfloat16), flip, preferred_element_type=jnp.float32)
 
     sub = lax.broadcasted_iota(jnp.int32, (8, LANE), 0)
     lane = lax.broadcasted_iota(jnp.int32, (8, LANE), 1)
@@ -104,7 +90,29 @@
                     ).astype(jnp.bfloat16)
         return carry
 
-    lax.fori_loop(0, groups, build, 0)
+    ahead = my_tmpl * 2 < peers
+    early = jnp.where(ahead, groups * 2 // 3 - jnp.minimum(my_tmpl, 1) * (groups // 3), 0)
+    pl.when(ahead)(prepare)
+    lax.fori_loop(0, early, build, 0)
+
+    pl.semaphore_wait(barrier, peers + owners - 2)
+
+    sends = []
+    for step in range(peers - 1):
+        target = step + jnp.where(my_tmpl <= step, 1, 0)
+        copy = pltpu.make_async_remote_copy(
+            src_ref=data_ref,
+            dst_ref=gathered.at[my_tmpl],
+            send_sem=data_send.at[step],
+            recv_sem=data_recv.at[my_tmpl],
+            device_id={"tmpl": target},
+            device_id_type=MESH,
+        )
+        copy.start()
+        sends.append(copy)
+
+    pl.when(jnp.logical_not(ahead))(prepare)
+    lax.fori_loop(early, groups, build, 0)
 
     fetches[1].wait()
     fetches[2].wait()

time: 17.3 us -> 16 us (0.925)
  Pallas kernels: 15.9 us -> 14.6 us
    pallas_call x1, Pallas kernels: 15.9 us -> 14.6 us  [shards(): pl.pallas_call(functools.partial(kernel, peers, owners), out_shape=jax.Sh...]
where the time goes in v2:
time: 16 us; the launch traced here: 15.9 us
  Pallas kernels  14.6 us (91%)
  local copies, waits for them, and re-layouts  1.26 us (8%)
    pallas_call x1, Pallas kernels, shards(): pl.pallas_call(functools.partial(kernel, peers, owners), out_shape=jax.Sh...  14.6 us
    unnamed x1, local copies, waits for them, and re-layouts  1.26 us

profile of v2, /device:TPU:0, one launch (start us, length us, event | category | flops | bytes accessed | tf_op | source)
XLA Modules:
  0.0 15.9 jit_solution(11347399988640343661)
XLA Ops:
  0.0 14.6 %shard_map.37 = f32[4,128]{1,0:T(4,128)} custom-call(s32[3,4,8]{2,1,0:T(4,128)} %bitcast.3, f32[3,8,320]{2,1,0:T(8,128)} %bitcast.2, bf16[8,3,4,256]{3,2,1,0:T(4,128)(2,1)} %templates_hbm.1), custom_call_target="tpu_custom_call" | custom-call | tf_op jit(solution)/shard_map/pallas_call | solution.py:222
  14.6 1.3 %copy.5 = f32[4,128]{1,0:T(4,128)} copy(f32[4,128]{1,0:T(4,128)} %shard_map.37) | data formatting | bytes 4096

commit v3 on v2

--- a/solution.py
+++ b/solution.py
@@ -182,8 +182,8 @@
         partial_ref[:, t, :] = same[:rows] + following[1 : rows + 1]
 
     span = LAGS // LANE // owners
-    for step in range(1, owners):
-        target = lax.rem(my_sta + step, owners)
+    for step in range(owners - 1):
+        target = step + jnp.where(my_sta <= step, 1, 0)
         copy = pltpu.make_async_remote_copy(
             src_ref=partial_ref.at[pl.ds(target * span, span)],
             dst_ref=arrived.at[my_sta],
@@ -243,7 +243,7 @@
             pltpu.SemaphoreType.DMA((owners,)),
         ],
         compiler_params=pltpu.CompilerParams(
-            collective_id=0, has_side_effects=True, vmem_limit_bytes=64 * 1024 * 1024
+            collective_id=0, has_side_effects=True, vmem_limit_bytes=64 * 1024 * 1024 - 10559488
         ),
     )(jnp.transpose(starts, (1, 2, 0)), jnp.transpose(data, (1, 0, 2)), templates)
 

time: 16 us -> 14.7 us (0.919)
  local copies, waits for them, and re-layouts: 1.26 us -> 0.58 us
  Pallas kernels: 14.6 us -> 14 us
    unnamed x1, local copies, waits for them, and re-layouts: 1.26 us -> 0.58 us
    pallas_call x1, Pallas kernels: 14.6 us -> 14 us  [shards(): pl.pallas_call(functools.partial(kernel, peers, owners), out_shape=jax.Sh...]
where the time goes in v3:
time: 14.7 us; the launch traced here: 14.6 us
  Pallas kernels  14 us (95%)
  local copies, waits for them, and re-layouts  0.58 us (4%)
    pallas_call x1, Pallas kernels, shards(): pl.pallas_call(functools.partial(kernel, peers, owners), out_shape=jax.Sh...  14 us
    unnamed x1, local copies, waits for them, and re-layouts  0.58 us

profile of v3, /device:TPU:0, one launch (start us, length us, event | category | flops | bytes accessed | tf_op | source)
XLA Modules:
  0.0 14.6 jit_solution(7825453121906146025)
XLA Ops:
  0.0 14.0 %shard_map.37 = f32[4,128]{1,0:T(4,128)S(1)} custom-call(s32[3,4,8]{2,1,0:T(4,128)} %bitcast.3, f32[3,8,320]{2,1,0:T(8,128)} %bitcast.2, bf16[8,3,4,256]{3,2,1,0:T(4,128)(2,1)} %templates_hbm.1), custom_call_target="tpu_custom_call" | custom-call | tf_op jit(solution)/shard_map/pallas_call | solution.py:222
  14.0 0.6 %copy.5 = f32[4,128]{1,0:T(4,128)} copy(f32[4,128]{1,0:T(4,128)S(1)} %shard_map.37) | data formatting | bytes 4096
